TPU v7x, 256 devices: a whole 4x4x8 slice. The times are simulated.
256 devices in a mesh: head: 4 (over x), grp: 4 (over y_hi, core), blk: 16 (over y_lo, z).
Axes of the slice: x: 4, y: 4 (y_hi: 2, y_lo: 2; y = y_hi * 2 + y_lo), z: 8, core: 2. Of those that a mesh axis runs over, the one named last changes fastest.
Arguments:
- tokens: bfloat16 [16384, 2880], P(('grp', 'blk'), 'head'), may hold values from -450 to 450
- norm_gain: float32 [2880], replicated, may hold values from 0.9 to 12
- w_query: bfloat16 [2880, 4096], P(None, 'head'), may hold values from -0.109375 to 0.109375
- w_key: bfloat16 [2880, 512], P(None, 'head'), may hold values from -0.109375 to 0.109375
- w_value: bfloat16 [2880, 512], P(None, 'head'), may hold values from -0.109375 to 0.109375
- sinks: float32 [64], P('head'), may hold values from 0 to 8
- doc_lengths: int32 [12], replicated, may hold values from 1 to 8192, 16384 in all
- tile_mask: int32 [128, 128], replicated, may hold values 0 or 1
Outputs:
- attended: bfloat16 [16384, 4096], P(('grp', 'blk'), 'head')
Inputs may be any that keep to these rules, and one draw needn't show every extreme that they name: `doc_lengths`: the 12 lengths sum to 16384 and the longest is exactly 8192.
All inputs are finite; a program needn't handle non-finite values.
Results may differ from a plain program's by a relative error of at most 0.017.
The roundings to bfloat16 on the way count: a program that leaves them out, or rounds other values in their place, can miss the bound.
Values may be sent and summed in bfloat16 or wider, within the bound.
A program may use at most 64 MiB of HBM per device.

v0:
```python
import jax
import jax.numpy as jnp
from jax import lax
from jax.sharding import PartitionSpec as P

HD = 64
TILE = 128


epsilon = 1e-05
rope_base = 150000.0


def sent_to_all(x, axis):
    length = lax.axis_size(axis)
    return lax.all_to_all(jnp.broadcast_to(x[None], (length, *x.shape)), axis, 0, 0, tiled=True)


def in_order(blocks, dim):
    dims = list(blocks.shape[1:])
    dims[dim] *= blocks.shape[0]
    return jnp.moveaxis(blocks, 0, dim).reshape(dims)


def gather_directly(x, axis, dim):
    blocks = sent_to_all(x, axis)
    return in_order(blocks, dim)


def shifted(x, axis, by):
    length = lax.axis_size(axis)
    return lax.ppermute(x, axis, [(i, (i + by) % length) for i in range(length)])


def from_behind(value, axis, steps):
    count = lax.axis_size(axis)
    leading, last = (max(0, -steps), min(count, count - steps))
    return lax.ppermute(value, axis, [(source, source + steps) for source in range(leading, last)])


def rotate(projected, positions, head_size):
    row_count = projected.shape[0]
    head_count = projected.shape[1] // head_size
    half_size = head_size // 2
    shaped = projected.reshape(row_count, head_count, head_size)
    frequency = rope_base ** (-2.0 * jnp.arange(half_size, dtype=jnp.float32) / head_size)
    angles = positions.astype(jnp.float32)[:, None] * frequency[None, :]
    cosine = jnp.cos(angles)[:, None, :]
    sine_part = jnp.sin(angles)[:, None, :]
    first_half = shaped[:, :, :half_size]
    second_half = shaped[:, :, half_size:]
    turned = jnp.concatenate(
        [
            first_half * cosine - second_half * sine_part,
            second_half * cosine + first_half * sine_part,
        ],
        axis=2,
    )
    return turned.reshape(row_count, head_count * head_size)


def doc_index(positions, doc_ends):
    return jnp.sum((doc_ends[None, :] <= positions[:, None]).astype(jnp.int32), axis=1)


def tile_rows(positions, tile_mask):
    tile_count = tile_mask.shape[0]
    selector = (
        positions[:, None] // TILE == jnp.arange(tile_count, dtype=jnp.int32)[None, :]
    ).astype(jnp.float32)
    return jnp.dot(selector, tile_mask.astype(jnp.float32), preferred_element_type=jnp.float32)


def allowed_pairs(query_pos, query_doc, query_tiles, key_pos, doc_ends):
    key_doc = doc_index(key_pos, doc_ends)
    tile_count = query_tiles.shape[1]
    selector = (
        key_pos[:, None] // TILE == jnp.arange(tile_count, dtype=jnp.int32)[None, :]
    ).astype(jnp.float32)
    listed = jnp.dot(query_tiles, selector.T, preferred_element_type=jnp.float32) > 0.5
    same_tile = query_pos[:, None] // TILE == key_pos[None, :] // TILE
    causal = key_pos[None, :] <= query_pos[:, None]
    return (query_doc[:, None] == key_doc[None, :]) & causal & (listed | same_tile)


def attend(carried, query_heads, key_block, value_block, allowed):
    score_scale = HD ** (-0.5)

    def accumulate(current):
        running_max, running_sum, weighted = current
        scores = (
            jnp.einsum("qgxd,kgd->qgxk", query_heads, key_block, preferred_element_type=jnp.float32)
            * score_scale
        )
        masked = jnp.where(allowed[:, None, None, :], scores, -1e30)
        new_max = jnp.maximum(running_max, jnp.max(masked, axis=3))
        weights = jnp.where(allowed[:, None, None, :], jnp.exp(masked - new_max[..., None]), 0.0)
        factor = jnp.exp(running_max - new_max)
        running_sum = running_sum * factor + jnp.sum(weights, axis=3)
        weighted = weighted * factor[..., None] + jnp.einsum(
            "qgxk,kgd->qgxd",
            weights.astype(jnp.bfloat16),
            value_block,
            preferred_element_type=jnp.float32,
        )
        return (new_max, running_sum, weighted)

    return lax.cond(jnp.any(allowed), accumulate, lambda current: current, carried)


def body(tokens, norm_gain, w_query, w_key, w_value, sinks, doc_lengths, tile_mask):
    gathered = gather_directly(tokens, "head", 1)
    widened = gathered.astype(jnp.float32)
    normed = (
        widened
        * lax.rsqrt(jnp.mean(widened * widened, axis=1, keepdims=True) + epsilon)
        * norm_gain[None, :]
    ).astype(jnp.bfloat16)
    row_count = tokens.shape[0]
    block_count = lax.axis_size("blk")
    group_count = lax.axis_size("grp")
    group_at = lax.axis_index("grp")
    block_at = lax.axis_index("blk")
    device_at = group_at * block_count + block_at
    offsets = jnp.arange(row_count, dtype=jnp.int32)
    own_pos = device_at * row_count + offsets
    queries = rotate(
        jnp.dot(normed, w_query, preferred_element_type=jnp.float32), own_pos, HD
    ).astype(jnp.bfloat16)
    key_rows = rotate(
        jnp.dot(normed, w_key, preferred_element_type=jnp.float32), own_pos, HD
    ).astype(jnp.bfloat16)
    value_rows = jnp.dot(normed, w_value, preferred_element_type=jnp.float32).astype(jnp.bfloat16)
    query_width = queries.shape[1]
    kv_width = key_rows.shape[1]
    kv_count = kv_width // HD
    per_group = query_width // kv_width
    doc_ends = jnp.cumsum(doc_lengths)
    sections = 1

    def locate(source):
        return source * row_count + offsets

    span = row_count // sections
    query_pos = locate(device_at)
    query_doc = doc_index(query_pos, doc_ends)
    query_tiles = tile_rows(query_pos, tile_mask)
    query_heads = queries.reshape(row_count, kv_count, per_group, HD)
    sink_heads = sinks.reshape(kv_count, per_group)
    carried = tuple(
        (
            (
                jnp.broadcast_to(sink_heads[None], (span, kv_count, per_group)),
                jnp.ones((span, kv_count, per_group), jnp.float32),
                jnp.zeros((span, kv_count, per_group, HD), jnp.float32),
            )
            for section in range(sections)
        )
    )
    key_value = jnp.concatenate([key_rows, value_rows], axis=1)

    def visit_block(current, key_value_in, source):
        key_pos = locate(source)
        allowed = allowed_pairs(query_pos, query_doc, query_tiles, key_pos, doc_ends)
        key_block = key_value_in[:, :kv_width].reshape(row_count, kv_count, HD)
        value_block = key_value_in[:, kv_width:].reshape(row_count, kv_count, HD)
        state = current[0]
        state = attend(state, query_heads, key_block, value_block, allowed)
        updated = [state]
        return tuple(updated)

    def round_trip(outer_turn, outer_carry):

        def cycle_hop(inner_turn, inner_carry):
            key_value_in, current = inner_carry
            source = (group_at - outer_turn) % group_count * block_count + (
                block_at - inner_turn
            ) % block_count
            current = visit_block(current, key_value_in, source)
            key_value_in = shifted(key_value_in, "blk", 1)
            return (key_value_in, current)

        key_value_in, current = lax.fori_loop(0, block_count, cycle_hop, outer_carry)
        key_value_in = from_behind(key_value_in, "grp", 1)
        return (key_value_in, current)

    key_value, carried = lax.fori_loop(0, group_count, round_trip, (key_value, carried))
    section = 0
    running_max, running_sum, weighted = carried[section]
    finished = (weighted / running_sum[..., None]).reshape(span, query_width)
    attended = finished.astype(jnp.bfloat16)
    return attended


def solution(mesh):
    in_specs = (
        P(("grp", "blk"), "head"),
        P(),
        P(None, "head"),
        P(None, "head"),
        P(None, "head"),
        P("head"),
        P(),
        P(),
    )
    out_specs = P(("grp", "blk"), "head")
    return jax.shard_map(body, mesh=mesh, in_specs=in_specs, out_specs=out_specs, check_vma=False)
```

profile of v0, /device:TPU:1, one launch (start us, length us, event | category | flops | bytes accessed | tf_op | source)
XLA Modules:
  0.0 590.3 jit_solution(13219646160733774402)
XLA Ops:
  2.3 4.8 all-to-all-start
  8.7 8.6 %copy.19 = bf16[2880,1024]{0,1:T(8,128)(2,1)} copy(bf16[2880,1024]{1,0:T(8,128)(2,1)} %param.16) | data formatting | bytes 11796480 | tf_op args[2]
  18.1 6.9 %all-to-all-done = bf16[4,256,720]{1,2,0:T(8,128)(2,1)S(1)} async-done(((bf16[4,256,720]{1,2,0:T(8,128)(2,1)}), bf16[4,256,720]{1,2,0:T(8,128)(2,1)S(1)}, u32[]{:S(2)}, u32[]{:S(2)}) %all-to-all-start) | async-done | bytes 1474592 | tf_op jit(solution)/shard_map/all_to_all | solution.py:16
  30.9 558.3 %while.77 = (s32[]{:T(128)}, bf16[256,256]{0,1:T(8,128)(2,1)S(1)}, f32[256,2,8]{0,2,1:T(8,128)S(1)}, f32[256,2,8]{0,2,1:T(8,128)S(1)}, f32[256,2,8,64]{0,3,2,1:T...) while((s32[]{:T(128)}, bf16[256,256]{0,1:T(8,128)(2,1)S(1)}, ...), condition=%wide.region_12.13_spmd.clone.clone, body=%wide.region_3.12_spmd.clone.clone.sunk | while | flops 299951104 | bytes 17781296 | solution.py:187
  31.0 116.8 %while.78 = (s32[]{:T(128)}, bf16[256,256]{0,1:T(8,128)(2,1)S(1)}, f32[256,2,8]{0,2,1:T(8,128)S(1)}, f32[256,2,8]{0,2,1:T(8,128)S(1)}, f32[256,2,8,64]{0,3,2,1:T...) while((s32[]{:T(128)}, bf16[256,256]{0,1:T(8,128)(2,1)S(1)}, ...), condition=%wide.region_11.11_spmd, body=%wide.region_4.10_spmd.sunk | while | flops 299950080 | bytes 16990224 | solution.py:183
  71.3 5.7 collective-permute-done
  79.4 5.3 collective-permute-done
  87.0 4.4 collective-permute-done
  100.6 4.4 collective-permute-done
  107.4 4.4 collective-permute-done
  114.2 4.4 collective-permute-done
  121.0 5.4 collective-permute-done
  128.7 5.5 collective-permute-done
  143.4 4.4 collective-permute-done
  147.8 23.7 %collective-permute-start.1 = (bf16[256,256]{0,1:T(8,128)(2,1)S(1)}, bf16[256,256]{0,1:T(8,128)(2,1)S(1)}, u32[]{:S(2)}, u32[]{:S(2)}) collective-permute-start(bf16[256,256]{0,1:T(8,128)(2,1)S(1)} %get-tuple-element.1277), channel_id=1, source_target_pairs={{0,16},{16,32},{32,48},{1,17},{17,33},{33,49},{2,18},{18,34},{34,5... | collective-permute-start | bytes 393224 | tf_op jit(solution)/shard_map/while/body/eval_jaxpr/ppermute | solution.py:38
  173.5 112.9 %while.78 = (s32[]{:T(128)}, bf16[256,256]{0,1:T(8,128)(2,1)S(1)}, f32[256,2,8]{0,2,1:T(8,128)S(1)}, f32[256,2,8]{0,2,1:T(8,128)S(1)}, f32[256,2,8,64]{0,3,2,1:T...) while((s32[]{:T(128)}, bf16[256,256]{0,1:T(8,128)(2,1)S(1)}, ...), condition=%wide.region_11.11_spmd, body=%wide.region_4.10_spmd.sunk | while | flops 299950080 | bytes 16990224 | solution.py:183
  175.9 4.4 collective-permute-done
  189.5 4.5 collective-permute-done
  196.3 5.7 collective-permute-done
  204.4 5.3 collective-permute-done
  212.1 4.4 collective-permute-done
  232.4 4.4 collective-permute-done
  239.2 4.4 collective-permute-done
  246.0 5.4 collective-permute-done
  253.7 5.5 collective-permute-done
  268.4 4.4 collective-permute-done
  275.2 4.4 collective-permute-done
  282.0 4.4 collective-permute-done
  286.4 23.7 %collective-permute-start.1 = (bf16[256,256]{0,1:T(8,128)(2,1)S(1)}, bf16[256,256]{0,1:T(8,128)(2,1)S(1)}, u32[]{:S(2)}, u32[]{:S(2)}) collective-permute-start(bf16[256,256]{0,1:T(8,128)(2,1)S(1)} %get-tuple-element.1277), channel_id=1, source_target_pairs={{0,16},{16,32},{32,48},{1,17},{17,33},{33,49},{2,18},{18,34},{34,5... | collective-permute-start | bytes 393224 | tf_op jit(solution)/shard_map/while/body/eval_jaxpr/ppermute | solution.py:38
  312.1 113.6 %while.78 = (s32[]{:T(128)}, bf16[256,256]{0,1:T(8,128)(2,1)S(1)}, f32[256,2,8]{0,2,1:T(8,128)S(1)}, f32[256,2,8]{0,2,1:T(8,128)S(1)}, f32[256,2,8,64]{0,3,2,1:T...) while((s32[]{:T(128)}, bf16[256,256]{0,1:T(8,128)(2,1)S(1)}, ...), condition=%wide.region_11.11_spmd, body=%wide.region_4.10_spmd.sunk | while | flops 299950080 | bytes 16990224 | solution.py:183
  314.5 4.5 collective-permute-done
  321.3 5.7 collective-permute-done
  329.4 5.3 collective-permute-done
  337.0 4.4 collective-permute-done
  343.8 4.4 collective-permute-done
  350.6 4.4 collective-permute-done
  357.4 4.4 collective-permute-done
  371.0 5.4 collective-permute-done
  378.7 5.5 collective-permute-done
  420.5 5.2 collective-permute-done
  425.7 23.0 %collective-permute-start.1 = (bf16[256,256]{0,1:T(8,128)(2,1)S(1)}, bf16[256,256]{0,1:T(8,128)(2,1)S(1)}, u32[]{:S(2)}, u32[]{:S(2)}) collective-permute-start(bf16[256,256]{0,1:T(8,128)(2,1)S(1)} %get-tuple-element.1277), channel_id=1, source_target_pairs={{0,16},{16,32},{32,48},{1,17},{17,33},{33,49},{2,18},{18,34},{34,5... | collective-permute-start | bytes 393224 | tf_op jit(solution)/shard_map/while/body/eval_jaxpr/ppermute | solution.py:38
  450.7 113.0 %while.78 = (s32[]{:T(128)}, bf16[256,256]{0,1:T(8,128)(2,1)S(1)}, f32[256,2,8]{0,2,1:T(8,128)S(1)}, f32[256,2,8]{0,2,1:T(8,128)S(1)}, f32[256,2,8,64]{0,3,2,1:T...) while((s32[]{:T(128)}, bf16[256,256]{0,1:T(8,128)(2,1)S(1)}, ...), condition=%wide.region_11.11_spmd, body=%wide.region_4.10_spmd.sunk | while | flops 299950080 | bytes 16990224 | solution.py:183
  487.0 5.4 collective-permute-done
  494.8 5.5 collective-permute-done
  536.6 5.2 collective-permute-done
  544.1 5.6 collective-permute-done
  552.1 4.8 collective-permute-done
  563.7 23.6 %collective-permute-start.1 = (bf16[256,256]{0,1:T(8,128)(2,1)S(1)}, bf16[256,256]{0,1:T(8,128)(2,1)S(1)}, u32[]{:S(2)}, u32[]{:S(2)}) collective-permute-start(bf16[256,256]{0,1:T(8,128)(2,1)S(1)} %get-tuple-element.1277), channel_id=1, source_target_pairs={{0,16},{16,32},{32,48},{1,17},{17,33},{33,49},{2,18},{18,34},{34,5... | collective-permute-start | bytes 393224 | tf_op jit(solution)/shard_map/while/body/eval_jaxpr/ppermute | solution.py:38
  (550 shorter events, 265.0 us)
Async XLA Ops:
  2.3 22.7 %all-to-all-start = ((bf16[4,256,720]{1,2,0:T(8,128)(2,1)}), bf16[4,256,720]{1,2,0:T(8,128)(2,1)S(1)}, u32[]{:S(2)}, u32[]{:S(2)}) async-start(bf16[4,256,720]{1,2,0:T(8,128)(2,1)} %broadcast_in_dim.42), calls=%async_computation | async-start | bytes 2949120 | tf_op jit(solution)/shard_map/all_to_all | solution.py:16
  31.7 10.1 %collective-permute-start = (bf16[256,256]{0,1:T(8,128)(2,1)}, bf16[256,256]{0,1:T(8,128)(2,1)S(1)}, u32[]{:S(2)}, u32[]{:S(2)}) collective-permute-start(bf16[256,256]{0,1:T(8,128)(2,1)} %copy.36), channel_id=1, source_target_pairs={{0,1},{1,2},{2,3},{3,4},{4,5},{5,6},{6,7},{7,8},{8,9},{9,10},{10,1... | collective-permute-start | bytes 393224 | tf_op jit(solution)/shard_map/while/body/eval_jaxpr/while/body/eval_jaxpr/ppermute | solution.py:32
  42.4 6.1 %collective-permute-start = (bf16[256,256]{0,1:T(8,128)(2,1)}, bf16[256,256]{0,1:T(8,128)(2,1)S(1)}, u32[]{:S(2)}, u32[]{:S(2)}) collective-permute-start(bf16[256,256]{0,1:T(8,128)(2,1)} %copy.36), channel_id=1, source_target_pairs={{0,1},{1,2},{2,3},{3,4},{4,5},{5,6},{6,7},{7,8},{8,9},{9,10},{10,1... | collective-permute-start | bytes 393224 | tf_op jit(solution)/shard_map/while/body/eval_jaxpr/while/body/eval_jaxpr/ppermute | solution.py:32
  49.2 6.1 %collective-permute-start = (bf16[256,256]{0,1:T(8,128)(2,1)}, bf16[256,256]{0,1:T(8,128)(2,1)S(1)}, u32[]{:S(2)}, u32[]{:S(2)}) collective-permute-start(bf16[256,256]{0,1:T(8,128)(2,1)} %copy.36), channel_id=1, source_target_pairs={{0,1},{1,2},{2,3},{3,4},{4,5},{5,6},{6,7},{7,8},{8,9},{9,10},{10,1... | collective-permute-start | bytes 393224 | tf_op jit(solution)/shard_map/while/body/eval_jaxpr/while/body/eval_jaxpr/ppermute | solution.py:32
  56.0 6.1 %collective-permute-start = (bf16[256,256]{0,1:T(8,128)(2,1)}, bf16[256,256]{0,1:T(8,128)(2,1)S(1)}, u32[]{:S(2)}, u32[]{:S(2)}) collective-permute-start(bf16[256,256]{0,1:T(8,128)(2,1)} %copy.36), channel_id=1, source_target_pairs={{0,1},{1,2},{2,3},{3,4},{4,5},{5,6},{6,7},{7,8},{8,9},{9,10},{10,1... | collective-permute-start | bytes 393224 | tf_op jit(solution)/shard_map/while/body/eval_jaxpr/while/body/eval_jaxpr/ppermute | solution.py:32
  62.8 6.2 %collective-permute-start = (bf16[256,256]{0,1:T(8,128)(2,1)}, bf16[256,256]{0,1:T(8,128)(2,1)S(1)}, u32[]{:S(2)}, u32[]{:S(2)}) collective-permute-start(bf16[256,256]{0,1:T(8,128)(2,1)} %copy.36), channel_id=1, source_target_pairs={{0,1},{1,2},{2,3},{3,4},{4,5},{5,6},{6,7},{7,8},{8,9},{9,10},{10,1... | collective-permute-start | bytes 393224 | tf_op jit(solution)/shard_map/while/body/eval_jaxpr/while/body/eval_jaxpr/ppermute | solution.py:32
  69.6 7.4 %collective-permute-start = (bf16[256,256]{0,1:T(8,128)(2,1)}, bf16[256,256]{0,1:T(8,128)(2,1)S(1)}, u32[]{:S(2)}, u32[]{:S(2)}) collective-permute-start(bf16[256,256]{0,1:T(8,128)(2,1)} %copy.36), channel_id=1, source_target_pairs={{0,1},{1,2},{2,3},{3,4},{4,5},{5,6},{6,7},{7,8},{8,9},{9,10},{10,1... | collective-permute-start | bytes 393224 | tf_op jit(solution)/shard_map/while/body/eval_jaxpr/while/body/eval_jaxpr/ppermute | solution.py:32
  77.7 7.0 %collective-permute-start = (bf16[256,256]{0,1:T(8,128)(2,1)}, bf16[256,256]{0,1:T(8,128)(2,1)S(1)}, u32[]{:S(2)}, u32[]{:S(2)}) collective-permute-start(bf16[256,256]{0,1:T(8,128)(2,1)} %copy.36), channel_id=1, source_target_pairs={{0,1},{1,2},{2,3},{3,4},{4,5},{5,6},{6,7},{7,8},{8,9},{9,10},{10,1... | collective-permute-start | bytes 393224 | tf_op jit(solution)/shard_map/while/body/eval_jaxpr/while/body/eval_jaxpr/ppermute | solution.py:32
  85.3 6.1 %collective-permute-start = (bf16[256,256]{0,1:T(8,128)(2,1)}, bf16[256,256]{0,1:T(8,128)(2,1)S(1)}, u32[]{:S(2)}, u32[]{:S(2)}) collective-permute-start(bf16[256,256]{0,1:T(8,128)(2,1)} %copy.36), channel_id=1, source_target_pairs={{0,1},{1,2},{2,3},{3,4},{4,5},{5,6},{6,7},{7,8},{8,9},{9,10},{10,1... | collective-permute-start | bytes 393224 | tf_op jit(solution)/shard_map/while/body/eval_jaxpr/while/body/eval_jaxpr/ppermute | solution.py:32
  92.1 6.1 %collective-permute-start = (bf16[256,256]{0,1:T(8,128)(2,1)}, bf16[256,256]{0,1:T(8,128)(2,1)S(1)}, u32[]{:S(2)}, u32[]{:S(2)}) collective-permute-start(bf16[256,256]{0,1:T(8,128)(2,1)} %copy.36), channel_id=1, source_target_pairs={{0,1},{1,2},{2,3},{3,4},{4,5},{5,6},{6,7},{7,8},{8,9},{9,10},{10,1... | collective-permute-start | bytes 393224 | tf_op jit(solution)/shard_map/while/body/eval_jaxpr/while/body/eval_jaxpr/ppermute | solution.py:32
  98.9 6.1 %collective-permute-start = (bf16[256,256]{0,1:T(8,128)(2,1)}, bf16[256,256]{0,1:T(8,128)(2,1)S(1)}, u32[]{:S(2)}, u32[]{:S(2)}) collective-permute-start(bf16[256,256]{0,1:T(8,128)(2,1)} %copy.36), channel_id=1, source_target_pairs={{0,1},{1,2},{2,3},{3,4},{4,5},{5,6},{6,7},{7,8},{8,9},{9,10},{10,1... | collective-permute-start | bytes 393224 | tf_op jit(solution)/shard_map/while/body/eval_jaxpr/while/body/eval_jaxpr/ppermute | solution.py:32
  105.7 6.1 %collective-permute-start = (bf16[256,256]{0,1:T(8,128)(2,1)}, bf16[256,256]{0,1:T(8,128)(2,1)S(1)}, u32[]{:S(2)}, u32[]{:S(2)}) collective-permute-start(bf16[256,256]{0,1:T(8,128)(2,1)} %copy.36), channel_id=1, source_target_pairs={{0,1},{1,2},{2,3},{3,4},{4,5},{5,6},{6,7},{7,8},{8,9},{9,10},{10,1... | collective-permute-start | bytes 393224 | tf_op jit(solution)/shard_map/while/body/eval_jaxpr/while/body/eval_jaxpr/ppermute | solution.py:32
  112.5 6.1 %collective-permute-start = (bf16[256,256]{0,1:T(8,128)(2,1)}, bf16[256,256]{0,1:T(8,128)(2,1)S(1)}, u32[]{:S(2)}, u32[]{:S(2)}) collective-permute-start(bf16[256,256]{0,1:T(8,128)(2,1)} %copy.36), channel_id=1, source_target_pairs={{0,1},{1,2},{2,3},{3,4},{4,5},{5,6},{6,7},{7,8},{8,9},{9,10},{10,1... | collective-permute-start | bytes 393224 | tf_op jit(solution)/shard_map/while/body/eval_jaxpr/while/body/eval_jaxpr/ppermute | solution.py:32
  119.3 7.1 %collective-permute-start = (bf16[256,256]{0,1:T(8,128)(2,1)}, bf16[256,256]{0,1:T(8,128)(2,1)S(1)}, u32[]{:S(2)}, u32[]{:S(2)}) collective-permute-start(bf16[256,256]{0,1:T(8,128)(2,1)} %copy.36), channel_id=1, source_target_pairs={{0,1},{1,2},{2,3},{3,4},{4,5},{5,6},{6,7},{7,8},{8,9},{9,10},{10,1... | collective-permute-start | bytes 393224 | tf_op jit(solution)/shard_map/while/body/eval_jaxpr/while/body/eval_jaxpr/ppermute | solution.py:32
  127.0 7.2 %collective-permute-start = (bf16[256,256]{0,1:T(8,128)(2,1)}, bf16[256,256]{0,1:T(8,128)(2,1)S(1)}, u32[]{:S(2)}, u32[]{:S(2)}) collective-permute-start(bf16[256,256]{0,1:T(8,128)(2,1)} %copy.36), channel_id=1, source_target_pairs={{0,1},{1,2},{2,3},{3,4},{4,5},{5,6},{6,7},{7,8},{8,9},{9,10},{10,1... | collective-permute-start | bytes 393224 | tf_op jit(solution)/shard_map/while/body/eval_jaxpr/while/body/eval_jaxpr/ppermute | solution.py:32
  134.9 6.1 %collective-permute-start = (bf16[256,256]{0,1:T(8,128)(2,1)}, bf16[256,256]{0,1:T(8,128)(2,1)S(1)}, u32[]{:S(2)}, u32[]{:S(2)}) collective-permute-start(bf16[256,256]{0,1:T(8,128)(2,1)} %copy.36), channel_id=1, source_target_pairs={{0,1},{1,2},{2,3},{3,4},{4,5},{5,6},{6,7},{7,8},{8,9},{9,10},{10,1... | collective-permute-start | bytes 393224 | tf_op jit(solution)/shard_map/while/body/eval_jaxpr/while/body/eval_jaxpr/ppermute | solution.py:32
  141.7 6.1 %collective-permute-start = (bf16[256,256]{0,1:T(8,128)(2,1)}, bf16[256,256]{0,1:T(8,128)(2,1)S(1)}, u32[]{:S(2)}, u32[]{:S(2)}) collective-permute-start(bf16[256,256]{0,1:T(8,128)(2,1)} %copy.36), channel_id=1, source_target_pairs={{0,1},{1,2},{2,3},{3,4},{4,5},{5,6},{6,7},{7,8},{8,9},{9,10},{10,1... | collective-permute-start | bytes 393224 | tf_op jit(solution)/shard_map/while/body/eval_jaxpr/while/body/eval_jaxpr/ppermute | solution.py:32
  147.8 25.6 %collective-permute-start.1 = (bf16[256,256]{0,1:T(8,128)(2,1)S(1)}, bf16[256,256]{0,1:T(8,128)(2,1)S(1)}, u32[]{:S(2)}, u32[]{:S(2)}) collective-permute-start(bf16[256,256]{0,1:T(8,128)(2,1)S(1)} %get-tuple-element.1277), channel_id=1, source_target_pairs={{0,16},{16,32},{32,48},{1,17},{17,33},{33,49},{2,18},{18,34},{34,5... | collective-permute-start | bytes 393224 | tf_op jit(solution)/shard_map/while/body/eval_jaxpr/ppermute | solution.py:38
  174.2 6.1 %collective-permute-start = (bf16[256,256]{0,1:T(8,128)(2,1)}, bf16[256,256]{0,1:T(8,128)(2,1)S(1)}, u32[]{:S(2)}, u32[]{:S(2)}) collective-permute-start(bf16[256,256]{0,1:T(8,128)(2,1)} %copy.36), channel_id=1, source_target_pairs={{0,1},{1,2},{2,3},{3,4},{4,5},{5,6},{6,7},{7,8},{8,9},{9,10},{10,1... | collective-permute-start | bytes 393224 | tf_op jit(solution)/shard_map/while/body/eval_jaxpr/while/body/eval_jaxpr/ppermute | solution.py:32
  181.0 6.1 %collective-permute-start = (bf16[256,256]{0,1:T(8,128)(2,1)}, bf16[256,256]{0,1:T(8,128)(2,1)S(1)}, u32[]{:S(2)}, u32[]{:S(2)}) collective-permute-start(bf16[256,256]{0,1:T(8,128)(2,1)} %copy.36), channel_id=1, source_target_pairs={{0,1},{1,2},{2,3},{3,4},{4,5},{5,6},{6,7},{7,8},{8,9},{9,10},{10,1... | collective-permute-start | bytes 393224 | tf_op jit(solution)/shard_map/while/body/eval_jaxpr/while/body/eval_jaxpr/ppermute | solution.py:32
  187.8 6.2 %collective-permute-start = (bf16[256,256]{0,1:T(8,128)(2,1)}, bf16[256,256]{0,1:T(8,128)(2,1)S(1)}, u32[]{:S(2)}, u32[]{:S(2)}) collective-permute-start(bf16[256,256]{0,1:T(8,128)(2,1)} %copy.36), channel_id=1, source_target_pairs={{0,1},{1,2},{2,3},{3,4},{4,5},{5,6},{6,7},{7,8},{8,9},{9,10},{10,1... | collective-permute-start | bytes 393224 | tf_op jit(solution)/shard_map/while/body/eval_jaxpr/while/body/eval_jaxpr/ppermute | solution.py:32
  194.6 7.4 %collective-permute-start = (bf16[256,256]{0,1:T(8,128)(2,1)}, bf16[256,256]{0,1:T(8,128)(2,1)S(1)}, u32[]{:S(2)}, u32[]{:S(2)}) collective-permute-start(bf16[256,256]{0,1:T(8,128)(2,1)} %copy.36), channel_id=1, source_target_pairs={{0,1},{1,2},{2,3},{3,4},{4,5},{5,6},{6,7},{7,8},{8,9},{9,10},{10,1... | collective-permute-start | bytes 393224 | tf_op jit(solution)/shard_map/while/body/eval_jaxpr/while/body/eval_jaxpr/ppermute | solution.py:32
  202.7 7.0 %collective-permute-start = (bf16[256,256]{0,1:T(8,128)(2,1)}, bf16[256,256]{0,1:T(8,128)(2,1)S(1)}, u32[]{:S(2)}, u32[]{:S(2)}) collective-permute-start(bf16[256,256]{0,1:T(8,128)(2,1)} %copy.36), channel_id=1, source_target_pairs={{0,1},{1,2},{2,3},{3,4},{4,5},{5,6},{6,7},{7,8},{8,9},{9,10},{10,1... | collective-permute-start | bytes 393224 | tf_op jit(solution)/shard_map/while/body/eval_jaxpr/while/body/eval_jaxpr/ppermute | solution.py:32
  210.4 6.1 %collective-permute-start = (bf16[256,256]{0,1:T(8,128)(2,1)}, bf16[256,256]{0,1:T(8,128)(2,1)S(1)}, u32[]{:S(2)}, u32[]{:S(2)}) collective-permute-start(bf16[256,256]{0,1:T(8,128)(2,1)} %copy.36), channel_id=1, source_target_pairs={{0,1},{1,2},{2,3},{3,4},{4,5},{5,6},{6,7},{7,8},{8,9},{9,10},{10,1... | collective-permute-start | bytes 393224 | tf_op jit(solution)/shard_map/while/body/eval_jaxpr/while/body/eval_jaxpr/ppermute | solution.py:32
  217.2 6.1 %collective-permute-start = (bf16[256,256]{0,1:T(8,128)(2,1)}, bf16[256,256]{0,1:T(8,128)(2,1)S(1)}, u32[]{:S(2)}, u32[]{:S(2)}) collective-permute-start(bf16[256,256]{0,1:T(8,128)(2,1)} %copy.36), channel_id=1, source_target_pairs={{0,1},{1,2},{2,3},{3,4},{4,5},{5,6},{6,7},{7,8},{8,9},{9,10},{10,1... | collective-permute-start | bytes 393224 | tf_op jit(solution)/shard_map/while/body/eval_jaxpr/while/body/eval_jaxpr/ppermute | solution.py:32
  223.9 6.1 %collective-permute-start = (bf16[256,256]{0,1:T(8,128)(2,1)}, bf16[256,256]{0,1:T(8,128)(2,1)S(1)}, u32[]{:S(2)}, u32[]{:S(2)}) collective-permute-start(bf16[256,256]{0,1:T(8,128)(2,1)} %copy.36), channel_id=1, source_target_pairs={{0,1},{1,2},{2,3},{3,4},{4,5},{5,6},{6,7},{7,8},{8,9},{9,10},{10,1... | collective-permute-start | bytes 393224 | tf_op jit(solution)/shard_map/while/body/eval_jaxpr/while/body/eval_jaxpr/ppermute | solution.py:32
  230.7 6.1 %collective-permute-start = (bf16[256,256]{0,1:T(8,128)(2,1)}, bf16[256,256]{0,1:T(8,128)(2,1)S(1)}, u32[]{:S(2)}, u32[]{:S(2)}) collective-permute-start(bf16[256,256]{0,1:T(8,128)(2,1)} %copy.36), channel_id=1, source_target_pairs={{0,1},{1,2},{2,3},{3,4},{4,5},{5,6},{6,7},{7,8},{8,9},{9,10},{10,1... | collective-permute-start | bytes 393224 | tf_op jit(solution)/shard_map/while/body/eval_jaxpr/while/body/eval_jaxpr/ppermute | solution.py:32
  237.5 6.1 %collective-permute-start = (bf16[256,256]{0,1:T(8,128)(2,1)}, bf16[256,256]{0,1:T(8,128)(2,1)S(1)}, u32[]{:S(2)}, u32[]{:S(2)}) collective-permute-start(bf16[256,256]{0,1:T(8,128)(2,1)} %copy.36), channel_id=1, source_target_pairs={{0,1},{1,2},{2,3},{3,4},{4,5},{5,6},{6,7},{7,8},{8,9},{9,10},{10,1... | collective-permute-start | bytes 393224 | tf_op jit(solution)/shard_map/while/body/eval_jaxpr/while/body/eval_jaxpr/ppermute | solution.py:32
  244.3 7.1 %collective-permute-start = (bf16[256,256]{0,1:T(8,128)(2,1)}, bf16[256,256]{0,1:T(8,128)(2,1)S(1)}, u32[]{:S(2)}, u32[]{:S(2)}) collective-permute-start(bf16[256,256]{0,1:T(8,128)(2,1)} %copy.36), channel_id=1, source_target_pairs={{0,1},{1,2},{2,3},{3,4},{4,5},{5,6},{6,7},{7,8},{8,9},{9,10},{10,1... | collective-permute-start | bytes 393224 | tf_op jit(solution)/shard_map/while/body/eval_jaxpr/while/body/eval_jaxpr/ppermute | solution.py:32
  252.0 7.2 %collective-permute-start = (bf16[256,256]{0,1:T(8,128)(2,1)}, bf16[256,256]{0,1:T(8,128)(2,1)S(1)}, u32[]{:S(2)}, u32[]{:S(2)}) collective-permute-start(bf16[256,256]{0,1:T(8,128)(2,1)} %copy.36), channel_id=1, source_target_pairs={{0,1},{1,2},{2,3},{3,4},{4,5},{5,6},{6,7},{7,8},{8,9},{9,10},{10,1... | collective-permute-start | bytes 393224 | tf_op jit(solution)/shard_map/while/body/eval_jaxpr/while/body/eval_jaxpr/ppermute | solution.py:32
  259.9 6.1 %collective-permute-start = (bf16[256,256]{0,1:T(8,128)(2,1)}, bf16[256,256]{0,1:T(8,128)(2,1)S(1)}, u32[]{:S(2)}, u32[]{:S(2)}) collective-permute-start(bf16[256,256]{0,1:T(8,128)(2,1)} %copy.36), channel_id=1, source_target_pairs={{0,1},{1,2},{2,3},{3,4},{4,5},{5,6},{6,7},{7,8},{8,9},{9,10},{10,1... | collective-permute-start | bytes 393224 | tf_op jit(solution)/shard_map/while/body/eval_jaxpr/while/body/eval_jaxpr/ppermute | solution.py:32
  266.7 6.1 %collective-permute-start = (bf16[256,256]{0,1:T(8,128)(2,1)}, bf16[256,256]{0,1:T(8,128)(2,1)S(1)}, u32[]{:S(2)}, u32[]{:S(2)}) collective-permute-start(bf16[256,256]{0,1:T(8,128)(2,1)} %copy.36), channel_id=1, source_target_pairs={{0,1},{1,2},{2,3},{3,4},{4,5},{5,6},{6,7},{7,8},{8,9},{9,10},{10,1... | collective-permute-start | bytes 393224 | tf_op jit(solution)/shard_map/while/body/eval_jaxpr/while/body/eval_jaxpr/ppermute | solution.py:32
  286.4 25.6 %collective-permute-start.1 = (bf16[256,256]{0,1:T(8,128)(2,1)S(1)}, bf16[256,256]{0,1:T(8,128)(2,1)S(1)}, u32[]{:S(2)}, u32[]{:S(2)}) collective-permute-start(bf16[256,256]{0,1:T(8,128)(2,1)S(1)} %get-tuple-element.1277), channel_id=1, source_target_pairs={{0,16},{16,32},{32,48},{1,17},{17,33},{33,49},{2,18},{18,34},{34,5... | collective-permute-start | bytes 393224 | tf_op jit(solution)/shard_map/while/body/eval_jaxpr/ppermute | solution.py:38
  312.8 6.2 %collective-permute-start = (bf16[256,256]{0,1:T(8,128)(2,1)}, bf16[256,256]{0,1:T(8,128)(2,1)S(1)}, u32[]{:S(2)}, u32[]{:S(2)}) collective-permute-start(bf16[256,256]{0,1:T(8,128)(2,1)} %copy.36), channel_id=1, source_target_pairs={{0,1},{1,2},{2,3},{3,4},{4,5},{5,6},{6,7},{7,8},{8,9},{9,10},{10,1... | collective-permute-start | bytes 393224 | tf_op jit(solution)/shard_map/while/body/eval_jaxpr/while/body/eval_jaxpr/ppermute | solution.py:32
  319.6 7.4 %collective-permute-start = (bf16[256,256]{0,1:T(8,128)(2,1)}, bf16[256,256]{0,1:T(8,128)(2,1)S(1)}, u32[]{:S(2)}, u32[]{:S(2)}) collective-permute-start(bf16[256,256]{0,1:T(8,128)(2,1)} %copy.36), channel_id=1, source_target_pairs={{0,1},{1,2},{2,3},{3,4},{4,5},{5,6},{6,7},{7,8},{8,9},{9,10},{10,1... | collective-permute-start | bytes 393224 | tf_op jit(solution)/shard_map/while/body/eval_jaxpr/while/body/eval_jaxpr/ppermute | solution.py:32
  327.7 7.0 %collective-permute-start = (bf16[256,256]{0,1:T(8,128)(2,1)}, bf16[256,256]{0,1:T(8,128)(2,1)S(1)}, u32[]{:S(2)}, u32[]{:S(2)}) collective-permute-start(bf16[256,256]{0,1:T(8,128)(2,1)} %copy.36), channel_id=1, source_target_pairs={{0,1},{1,2},{2,3},{3,4},{4,5},{5,6},{6,7},{7,8},{8,9},{9,10},{10,1... | collective-permute-start | bytes 393224 | tf_op jit(solution)/shard_map/while/body/eval_jaxpr/while/body/eval_jaxpr/ppermute | solution.py:32
  362.5 6.1 %collective-permute-start = (bf16[256,256]{0,1:T(8,128)(2,1)}, bf16[256,256]{0,1:T(8,128)(2,1)S(1)}, u32[]{:S(2)}, u32[]{:S(2)}) collective-permute-start(bf16[256,256]{0,1:T(8,128)(2,1)} %copy.36), channel_id=1, source_target_pairs={{0,1},{1,2},{2,3},{3,4},{4,5},{5,6},{6,7},{7,8},{8,9},{9,10},{10,1... | collective-permute-start | bytes 393224 | tf_op jit(solution)/shard_map/while/body/eval_jaxpr/while/body/eval_jaxpr/ppermute | solution.py:32
  369.3 7.1 %collective-permute-start = (bf16[256,256]{0,1:T(8,128)(2,1)}, bf16[256,256]{0,1:T(8,128)(2,1)S(1)}, u32[]{:S(2)}, u32[]{:S(2)}) collective-permute-start(bf16[256,256]{0,1:T(8,128)(2,1)} %copy.36), channel_id=1, source_target_pairs={{0,1},{1,2},{2,3},{3,4},{4,5},{5,6},{6,7},{7,8},{8,9},{9,10},{10,1... | collective-permute-start | bytes 393224 | tf_op jit(solution)/shard_map/while/body/eval_jaxpr/while/body/eval_jaxpr/ppermute | solution.py:32
  377.0 7.2 %collective-permute-start = (bf16[256,256]{0,1:T(8,128)(2,1)}, bf16[256,256]{0,1:T(8,128)(2,1)S(1)}, u32[]{:S(2)}, u32[]{:S(2)}) collective-permute-start(bf16[256,256]{0,1:T(8,128)(2,1)} %copy.36), channel_id=1, source_target_pairs={{0,1},{1,2},{2,3},{3,4},{4,5},{5,6},{6,7},{7,8},{8,9},{9,10},{10,1... | collective-permute-start | bytes 393224 | tf_op jit(solution)/shard_map/while/body/eval_jaxpr/while/body/eval_jaxpr/ppermute | solution.py:32
  418.8 6.9 %collective-permute-start = (bf16[256,256]{0,1:T(8,128)(2,1)}, bf16[256,256]{0,1:T(8,128)(2,1)S(1)}, u32[]{:S(2)}, u32[]{:S(2)}) collective-permute-start(bf16[256,256]{0,1:T(8,128)(2,1)} %copy.36), channel_id=1, source_target_pairs={{0,1},{1,2},{2,3},{3,4},{4,5},{5,6},{6,7},{7,8},{8,9},{9,10},{10,1... | collective-permute-start | bytes 393224 | tf_op jit(solution)/shard_map/while/body/eval_jaxpr/while/body/eval_jaxpr/ppermute | solution.py:32
  425.7 24.9 %collective-permute-start.1 = (bf16[256,256]{0,1:T(8,128)(2,1)S(1)}, bf16[256,256]{0,1:T(8,128)(2,1)S(1)}, u32[]{:S(2)}, u32[]{:S(2)}) collective-permute-start(bf16[256,256]{0,1:T(8,128)(2,1)S(1)} %get-tuple-element.1277), channel_id=1, source_target_pairs={{0,16},{16,32},{32,48},{1,17},{17,33},{33,49},{2,18},{18,34},{34,5... | collective-permute-start | bytes 393224 | tf_op jit(solution)/shard_map/while/body/eval_jaxpr/ppermute | solution.py:38
  458.2 6.1 %collective-permute-start = (bf16[256,256]{0,1:T(8,128)(2,1)}, bf16[256,256]{0,1:T(8,128)(2,1)S(1)}, u32[]{:S(2)}, u32[]{:S(2)}) collective-permute-start(bf16[256,256]{0,1:T(8,128)(2,1)} %copy.36), channel_id=1, source_target_pairs={{0,1},{1,2},{2,3},{3,4},{4,5},{5,6},{6,7},{7,8},{8,9},{9,10},{10,1... | collective-permute-start | bytes 393224 | tf_op jit(solution)/shard_map/while/body/eval_jaxpr/while/body/eval_jaxpr/ppermute | solution.py:32
  485.3 7.1 %collective-permute-start = (bf16[256,256]{0,1:T(8,128)(2,1)}, bf16[256,256]{0,1:T(8,128)(2,1)S(1)}, u32[]{:S(2)}, u32[]{:S(2)}) collective-permute-start(bf16[256,256]{0,1:T(8,128)(2,1)} %copy.36), channel_id=1, source_target_pairs={{0,1},{1,2},{2,3},{3,4},{4,5},{5,6},{6,7},{7,8},{8,9},{9,10},{10,1... | collective-permute-start | bytes 393224 | tf_op jit(solution)/shard_map/while/body/eval_jaxpr/while/body/eval_jaxpr/ppermute | solution.py:32
  493.1 7.2 %collective-permute-start = (bf16[256,256]{0,1:T(8,128)(2,1)}, bf16[256,256]{0,1:T(8,128)(2,1)S(1)}, u32[]{:S(2)}, u32[]{:S(2)}) collective-permute-start(bf16[256,256]{0,1:T(8,128)(2,1)} %copy.36), channel_id=1, source_target_pairs={{0,1},{1,2},{2,3},{3,4},{4,5},{5,6},{6,7},{7,8},{8,9},{9,10},{10,1... | collective-permute-start | bytes 393224 | tf_op jit(solution)/shard_map/while/body/eval_jaxpr/while/body/eval_jaxpr/ppermute | solution.py:32
  534.9 6.9 %collective-permute-start = (bf16[256,256]{0,1:T(8,128)(2,1)}, bf16[256,256]{0,1:T(8,128)(2,1)S(1)}, u32[]{:S(2)}, u32[]{:S(2)}) collective-permute-start(bf16[256,256]{0,1:T(8,128)(2,1)} %copy.36), channel_id=1, source_target_pairs={{0,1},{1,2},{2,3},{3,4},{4,5},{5,6},{6,7},{7,8},{8,9},{9,10},{10,1... | collective-permute-start | bytes 393224 | tf_op jit(solution)/shard_map/while/body/eval_jaxpr/while/body/eval_jaxpr/ppermute | solution.py:32
  542.4 7.3 %collective-permute-start = (bf16[256,256]{0,1:T(8,128)(2,1)}, bf16[256,256]{0,1:T(8,128)(2,1)S(1)}, u32[]{:S(2)}, u32[]{:S(2)}) collective-permute-start(bf16[256,256]{0,1:T(8,128)(2,1)} %copy.36), channel_id=1, source_target_pairs={{0,1},{1,2},{2,3},{3,4},{4,5},{5,6},{6,7},{7,8},{8,9},{9,10},{10,1... | collective-permute-start | bytes 393224 | tf_op jit(solution)/shard_map/while/body/eval_jaxpr/while/body/eval_jaxpr/ppermute | solution.py:32
  550.4 6.5 %collective-permute-start = (bf16[256,256]{0,1:T(8,128)(2,1)}, bf16[256,256]{0,1:T(8,128)(2,1)S(1)}, u32[]{:S(2)}, u32[]{:S(2)}) collective-permute-start(bf16[256,256]{0,1:T(8,128)(2,1)} %copy.36), channel_id=1, source_target_pairs={{0,1},{1,2},{2,3},{3,4},{4,5},{5,6},{6,7},{7,8},{8,9},{9,10},{10,1... | collective-permute-start | bytes 393224 | tf_op jit(solution)/shard_map/while/body/eval_jaxpr/while/body/eval_jaxpr/ppermute | solution.py:32
  563.7 25.5 %collective-permute-start.1 = (bf16[256,256]{0,1:T(8,128)(2,1)S(1)}, bf16[256,256]{0,1:T(8,128)(2,1)S(1)}, u32[]{:S(2)}, u32[]{:S(2)}) collective-permute-start(bf16[256,256]{0,1:T(8,128)(2,1)S(1)} %get-tuple-element.1277), channel_id=1, source_target_pairs={{0,16},{16,32},{32,48},{1,17},{17,33},{33,49},{2,18},{18,34},{34,5... | collective-permute-start | bytes 393224 | tf_op jit(solution)/shard_map/while/body/eval_jaxpr/ppermute | solution.py:38
  (27 other events, 195.5 us)
where the time goes:
time: 595 us; the launch traced here: 590 us
  waiting for transfers between devices  308 us (52%)
  starting transfers between devices  103 us (17%)
  matrix products  65.6 us (11%)
  local copies, waits for them, and re-layouts  58.9 us (10%)
  loops' own time  43 us (7%)
  other arithmetic  12 us (2%)
    ppermute x64, waiting for transfers between devices, shifted(): lax.ppermute(x, axis, [(i, (i + by) % length) for i in range(length)])  293 us
    ppermute x4, starting transfers between devices, from_behind(): lax.ppermute(value, axis, [(source, source + steps) for source in range(l...  93.9 us
    dot_general x64, matrix products, allowed_pairs(): jnp.dot(query_tiles, selector.T, preferred_element_type=jnp.float32) > 0.5  58.6 us
    another operation x64, local copies, waits for them, and re-layouts  41.9 us
    another operation x4, loops' own time, round_trip(): lax.fori_loop(0, block_count, cycle_hop, outer_carry)  41.6 us
  transfers between devices with their start and end apart: 69, of which 69 were waited for; matrix products, arithmetic and copies ran while one was open for 14% of the time, Pallas kernels for 0%

commit v1 on v0

v1 whole, which is shorter than its diff:
```python
import functools

import jax
import jax.numpy as jnp
from jax import lax
from jax.experimental import pallas as pl
from jax.experimental.pallas import tpu as pltpu
from jax.sharding import PartitionSpec as P

MESH = pl.DeviceIdType.MESH
HD = 64
TILE = 128
ROWS = 256
NT = 128
CH = 4
EPS = 1e-05
ROPE_BASE = 150000.0
BF = jnp.bfloat16
F32 = jnp.float32


def place():
    h = lax.axis_index("head")
    g = lax.axis_index("grp")
    b = lax.axis_index("blk")
    c = g % 2
    y = (g // 2) * 2 + b // 8
    z = b % 8
    return h, g, b, c, y, z


def member(i, low):
    core, half, flip = i // 4, (i // 2) % 2, i % 2
    grp = half * 2 + core
    blk = low * (1 - flip) + (15 - low) * flip
    return grp, blk


def low_of(b):
    flip = b // 8
    return b * (1 - flip) + (15 - b) * flip


def own_member(g, b):
    return (g % 2) * 4 + (g // 2) * 2 + b // 8


def shard_id(yy, zz, core):
    return (yy // 2) * 32 + core * 16 + (yy % 2) * 8 + zz


def turned(x, cos, sin):
    lane = lax.broadcasted_iota(jnp.int32, x.shape, 1)
    other = jnp.where(lane % 64 < 32, pltpu.roll(x, 96, 1), pltpu.roll(x, 32, 1))
    return x * cos + other * sin


def project_kernel(
    tok, gain, cos, sin, wq_hbm, wk_hbm, wv_hbm,
    kv_out, q_out,
    xb, wq, wkv, kvs, qs,
    wsem, xs_sem, xr_sem, ks_sem, kr_sem, ps_sem, qs_sem, qr_sem,
):
    h, g, b, c, y, z = place()
    me = own_member(g, b)
    low = low_of(b)
    feats = tok.shape[1]

    copies_w = [
        pltpu.make_async_copy(wk_hbm, wkv.at[:, 0:128], wsem.at[0]),
        pltpu.make_async_copy(wv_hbm, wkv.at[:, 128:256], wsem.at[1]),
        pltpu.make_async_copy(wq_hbm, wq, wsem.at[2]),
    ]
    for cp in copies_w:
        cp.start()

    def plane(dy, dz):
        yy = (y + dy + 4) % 4
        zz = (z + dz + 8) % 8
        return {"grp": (yy // 2) * 2 + c, "blk": (yy % 2) * 8 + zz}

    partner = {"grp": (g // 2) * 2 + 1 - c}
    barrier = pltpu.get_barrier_semaphore()
    for d in range(1, 4):
        pl.semaphore_signal(barrier, inc=1, device_id={"head": (h + d) % 4}, device_id_type=MESH)
    for dy, dz in ((1, 0), (-1, 0), (0, 1), (0, -1)):
        pl.semaphore_signal(barrier, inc=1, device_id=plane(dy, dz), device_id_type=MESH)
    for d in range(1, 8):
        grp, blk = member((me + d) % 8, low)
        pl.semaphore_signal(barrier, inc=1, device_id={"grp": grp, "blk": blk}, device_id_type=MESH)
    pl.semaphore_wait(barrier, 14)

    sent = []
    for d in (1, 3, 2):
        cp = pltpu.make_async_remote_copy(
            tok, xb.at[h], xs_sem.at[d - 1], xr_sem.at[d - 1],
            device_id={"head": (h + d) % 4}, device_id_type=MESH)
        cp.start()
        sent.append(cp)
    xb[h] = tok[...]
    for cp in sent:
        cp.wait_recv()

    total = jnp.zeros((ROWS, 1), F32)
    for i in range(4):
        w = xb[i].astype(F32)
        total = total + jnp.sum(w * w, axis=1, keepdims=True)
    scale = lax.rsqrt(total / (4 * feats) + EPS)
    for i in range(4):
        w = xb[i].astype(F32) * scale * gain[:, i * feats:(i + 1) * feats]
        xb[i] = w.astype(BF)

    copies_w[0].wait()
    copies_w[1].wait()
    kvp = jnp.zeros((ROWS, 256), F32)
    for i in range(4):
        kvp = kvp + jnp.dot(xb[i], wkv[i * feats:(i + 1) * feats, :], preferred_element_type=F32)
    k = turned(kvp[:, :128], cos[...], sin[...])
    v = kvp[:, 128:]
    lane = lax.broadcasted_iota(jnp.int32, (128, 128), 1)
    k0, k1 = k[:128], k[128:]
    kvs[0, 0:128, :] = jnp.where(lane < 64, k0, pltpu.roll(k1, 64, 1)).astype(BF)
    kvs[1, 0:128, :] = jnp.where(lane < 64, pltpu.roll(k0, 64, 1), k1).astype(BF)
    for e in range(2):
        vt = v[128 * e:128 * (e + 1)].T.astype(BF)
        for cc in range(2):
            kvs[cc, 128 + 64 * e:192 + 64 * e, :] = vt[64 * cc:64 * (cc + 1)]
    own = shard_id(y, z, c)
    other = shard_id(y, z, 1 - c)
    pcopy = pltpu.make_async_remote_copy(
        kvs.at[1 - c], kv_out.at[own], ps_sem, kr_sem.at[own], device_id=partner, device_id_type=MESH)
    pcopy.start()
    kv_out[own] = kvs[c]

    sends = []

    def send(sid, target):
        cp = pltpu.make_async_remote_copy(
            kv_out.at[sid], kv_out.at[sid], ks_sem.at[len(sends)], kr_sem.at[sid],
            device_id=target, device_id_type=MESH)
        cp.start()
        sends.append(cp)

    def arrived(sid):
        pltpu.make_async_remote_copy(
            kv_out.at[sid], kv_out.at[sid], ps_sem, kr_sem.at[sid],
            device_id=partner, device_id_type=MESH).wait_recv()

    def block(dy, dz, core):
        return shard_id((y + dy + 4) % 4, (z + dz + 8) % 8, core)

    arrived(other)
    a0, b0 = block(0, 0, 0), block(0, 0, 1)
    for sid in (a0, b0):
        for dy, dz in ((0, 1), (0, -1), (1, 0), (-1, 0)):
            send(sid, plane(dy, dz))

    copies_w[2].wait()

    def q_block(n, carry):
        acc = jnp.zeros((ROWS, 256), F32)
        cols = pl.ds(pl.multiple_of(n * 256, 256), 256)
        for i in range(4):
            acc = acc + jnp.dot(xb[i], wq[i * feats:(i + 1) * feats, cols], preferred_element_type=F32)
        for u in range(2):
            qs[n * 2 + u] = (turned(acc[:, u * 128:(u + 1) * 128], cos[...], sin[...]) * 0.125).astype(BF)
        return carry

    lax.fori_loop(0, 4, q_block, 0)
    qsent = []
    for d in range(1, 8):
        i = (me + d) % 8
        grp, blk = member(i, low)
        cp = pltpu.make_async_remote_copy(
            qs.at[i], q_out.at[me], qs_sem.at[d - 1], qr_sem.at[d - 1],
            device_id={"grp": grp, "blk": blk}, device_id_type=MESH)
        cp.start()
        qsent.append(cp)
    q_out[me] = qs[me]

    events = []
    for dz in range(-4, 4):
        for dy in (0, -1, 1, 2):
            if (dy, dz) != (0, 0):
                events.append((abs(dz) + abs(dy), 0, dy, dz))
    for dz in range(-3, 5):
        for dy in (0, -1, 1, 2):
            if (dy, dz) != (0, 0):
                events.append((abs(dz) + abs(dy), 1, dy, dz))
    events.sort(key=lambda e: e[0])
    for hops, part, dy, dz in events:
        sid = block(dy, dz, part)
        arrived(sid)
        if part == 0:
            if dy == 0:
                if dz < 0 and dz > -4:
                    send(sid, plane(0, 1))
                if dz > 0 and dz < 3:
                    send(sid, plane(0, -1))
                send(sid, plane(1, 0))
                send(sid, plane(-1, 0))
            elif dy == -1 and dz % 2 == 0:
                send(sid, plane(1, 0))
            elif dy == 1 and dz % 2 == 1:
                send(sid, plane(-1, 0))
        else:
            if dz == 0:
                send(sid, plane(0, 1))
                send(sid, plane(0, -1))
                if dy == 1:
                    sgn = 1 - 2 * c
                    yy = (y - sgn + 4) % 4
                    send(shard_id(yy, z, 1), plane(sgn, 0))
            elif dz > 0 and dz < 4:
                send(sid, plane(0, -1))
            elif dz < 0 and dz > -3:
                send(sid, plane(0, 1))

    for cp in qsent:
        cp.wait_recv()
    for cp in sent + sends + qsent + [pcopy]:
        cp.wait_send()


def attend_kernel(meta, ends, sinks, q_ref, kv_ref, o_ref, qsel):
    lane = lax.broadcasted_iota(jnp.int32, (1, 256), 1)
    sub = lax.broadcasted_iota(jnp.int32, (TILE, 256), 0)
    base = meta[0, 123]
    sink = jnp.where(lane < 128, sinks[base], sinks[base + 1])

    def one_tile(n, carry0):
        m_idx = n // 2
        e = n % 2
        tile = meta[n, 120]
        nch = meta[n, 121]
        nf = meta[n, 122]
        qt = q_ref[m_idx, pl.ds(pl.multiple_of(e * 128, 128), 128), :].astype(F32).T.astype(BF)
        qt = jnp.concatenate([qt[:64], qt[64:]], axis=1)
        zero = jnp.zeros_like(qt)
        qsel[0] = jnp.concatenate([qt, zero], axis=0)
        qsel[1] = jnp.concatenate([zero, qt], axis=0)
        qpos = tile * TILE + lane % 128
        first = jnp.zeros_like(qpos)
        for d in range(12):
            first = jnp.maximum(first, jnp.where(ends[d] <= qpos, ends[d], 0))

        def step(ci, carry, masked):
            mx, den, acc = carry
            parts, vts = [], []
            for u in range(CH):
                j = meta[n, ci * CH + u]
                jj = j % 128
                s = jj // 2
                par = jj % 2
                sc = jnp.dot(kv_ref[s, 0:128, :], qsel[par], preferred_element_type=F32)
                if masked:
                    kpos = sub + j * TILE
                    sc = jnp.where((kpos <= qpos) & (kpos >= first), sc, -1e30)
                parts.append(sc)
                vts.append(kv_ref[s, pl.ds(pl.multiple_of(128 + 64 * par, 64), 64), :])
            sc = jnp.concatenate(parts, axis=0)
            vt = jnp.concatenate(vts, axis=1)
            new = jnp.maximum(mx, jnp.max(sc, axis=0, keepdims=True))
            p = jnp.exp(sc - new)
            alpha = jnp.exp(mx - new)
            den = den * alpha + jnp.sum(p, axis=0, keepdims=True)
            acc = acc * alpha + jnp.dot(vt, p.astype(BF), preferred_element_type=F32)
            return new, den, acc

        carry = (sink, jnp.ones((1, 256), F32), jnp.zeros((64, 256), F32))
        carry = step(0, carry, True)
        carry = lax.fori_loop(1, nf, lambda ci, cr: step(ci, cr, False), carry)
        carry = lax.fori_loop(jnp.maximum(1, nf), nch, lambda ci, cr: step(ci, cr, True), carry)
        _, den, acc = carry
        out = acc / den
        out = jnp.concatenate([out[:, :128], out[:, 128:]], axis=0)
        o_ref[m_idx, pl.ds(pl.multiple_of(e * 128, 128), 128), :] = out.T.astype(BF)
        return carry0

    lax.fori_loop(0, 16, one_tile, 0)


def return_kernel(o_ref, out_ref, s_sem, r_sem):
    h, g, b, c, y, z = place()
    me = own_member(g, b)
    low = low_of(b)
    barrier = pltpu.get_barrier_semaphore()
    for d in range(1, 8):
        grp, blk = member((me + d) % 8, low)
        pl.semaphore_signal(barrier, inc=1, device_id={"grp": grp, "blk": blk}, device_id_type=MESH)
    pl.semaphore_wait(barrier, 7)
    cols = pl.ds(pl.multiple_of(me * 128, 128), 128)
    sent = []
    for d in range(1, 8):
        i = (me + d) % 8
        grp, blk = member(i, low)
        cp = pltpu.make_async_remote_copy(
            o_ref.at[i], out_ref.at[:, cols], s_sem.at[d - 1], r_sem.at[d - 1],
            device_id={"grp": grp, "blk": blk}, device_id_type=MESH)
        cp.start()
        sent.append(cp)
    out_ref[:, cols] = o_ref[me]
    for cp in sent:
        cp.wait()


def key_lists(doc_lengths, tile_mask):
    g = lax.axis_index("grp")
    b = lax.axis_index("blk")
    low = low_of(b)
    i = jnp.arange(16, dtype=jnp.int32) // 2
    e = jnp.arange(16, dtype=jnp.int32) % 2
    grp, blk = member(i, low)
    tile = (grp * 16 + blk) * 2 + e
    ends = jnp.cumsum(doc_lengths).astype(jnp.int32)

    def start_of(p):
        return jnp.max(jnp.where(ends[None, :] <= p[:, None], ends[None, :], 0), axis=1)

    first = start_of(tile * TILE)
    last = start_of(tile * TILE + TILE - 1)
    j = jnp.arange(NT, dtype=jnp.int32)
    pick = (tile[:, None] == j[None, :]).astype(F32)
    rows = jnp.dot(pick, tile_mask.astype(F32), preferred_element_type=F32) > 0.5
    active = (rows | (j[None, :] == tile[:, None])) & (j[None, :] <= tile[:, None]) & (j[None, :] >= (first // TILE)[:, None])
    act = active.astype(F32)
    later = (j[:, None] > j[None, :]).astype(F32)
    behind = jnp.dot(act, later, preferred_element_type=F32).astype(jnp.int32)
    n = jnp.sum(active.astype(jnp.int32), axis=1)
    pad = (CH - n % CH) % CH
    pos = jnp.where(active, behind + pad[:, None], -1)
    hit = pos[:, :, None] == j[None, None, :]
    lists = jnp.sum(jnp.where(hit, j[None, :, None], 0), axis=1)
    lists = jnp.where(j[None, :] < pad[:, None], 128, lists)
    nch = (n + pad) // CH
    nf = jnp.where(first == last, nch - 1, 1)
    me = own_member(g, b)
    for col, val in ((120, tile), (121, nch), (122, nf), (123, jnp.full((16,), me * 2, jnp.int32))):
        lists = jnp.where(j[None, :] == col, val[:, None], lists)
    return lists, ends


def body(tokens, norm_gain, w_query, w_key, w_value, sinks, doc_lengths, tile_mask):
    g = lax.axis_index("grp")
    b = lax.axis_index("blk")
    pos = (g * 16 + b) * ROWS + jnp.arange(ROWS, dtype=jnp.int32)
    half = HD // 2
    freq = ROPE_BASE ** (-2.0 * jnp.arange(half, dtype=F32) / HD)
    ang = pos.astype(F32)[:, None] * freq[None, :]
    cos1, sin1 = jnp.cos(ang), jnp.sin(ang)
    cos = jnp.concatenate([cos1] * 4, axis=1)
    sin = jnp.concatenate([-sin1, sin1, -sin1, sin1], axis=1)
    lists, ends = key_lists(doc_lengths, tile_mask)

    vm = pl.BlockSpec(memory_space=pltpu.VMEM)
    anym = pl.BlockSpec(memory_space=pl.ANY)
    smem = pl.BlockSpec(memory_space=pltpu.SMEM)
    feats = tokens.shape[1]
    dma = pltpu.SemaphoreType.DMA
    kv, q = pl.pallas_call(
        project_kernel,
        out_shape=(jax.ShapeDtypeStruct((64, 256, 128), BF), jax.ShapeDtypeStruct((8, 256, 128), BF)),
        in_specs=[vm, vm, vm, vm, anym, anym, anym],
        out_specs=(vm, vm),
        scratch_shapes=[
            pltpu.VMEM((4, ROWS, feats), BF),
            pltpu.VMEM((4 * feats, 1024), BF),
            pltpu.VMEM((4 * feats, 256), BF),
            pltpu.VMEM((2, 256, 128), BF),
            pltpu.VMEM((8, 256, 128), BF),
            dma((3,)), dma((3,)), dma((3,)), dma((64,)), dma((64,)), dma, dma((7,)), dma((7,)),
        ],
        compiler_params=pltpu.CompilerParams(collective_id=0, has_side_effects=True),
        name="project",
    )(tokens, norm_gain[None, :], cos, sin, w_query, w_key, w_value)
    o = pl.pallas_call(
        attend_kernel,
        out_shape=jax.ShapeDtypeStruct((8, 256, 128), BF),
        in_specs=[smem, smem, smem, vm, vm],
        out_specs=vm,
        scratch_shapes=[pltpu.VMEM((2, 128, 256), BF)],
        name="attend",
    )(lists, ends, sinks, q, kv)
    return pl.pallas_call(
        return_kernel,
        out_shape=jax.ShapeDtypeStruct((ROWS, 1024), BF),
        in_specs=[vm],
        out_specs=vm,
        scratch_shapes=[dma((7,)), dma((7,))],
        compiler_params=pltpu.CompilerParams(collective_id=1, has_side_effects=True),
        name="give_back",
    )(o)


def solution(mesh):
    in_specs = (
        P(("grp", "blk"), "head"),
        P(),
        P(None, "head"),
        P(None, "head"),
        P(None, "head"),
        P("head"),
        P(),
        P(),
    )
    out_specs = P(("grp", "blk"), "head")
    return jax.shard_map(body, mesh=mesh, in_specs=in_specs, out_specs=out_specs, check_vma=False)
```

time: 595 us -> 148 us (0.25)
  the two profiles are of different devices: /device:TPU:1 before, /device:TPU:9 now
where the time goes in v1:
time: 148 us; the launch traced here: 150 us
  Pallas kernels  140 us (95%)
  local copies, waits for them, and re-layouts  5.09 us (3%)
  other arithmetic  3.71 us (3%)
    pallas_call x1, Pallas kernels, body(): pl.pallas_call(project_kernel, out_shape=(jax.ShapeDtypeStruct((64, 256,...  76.2 us
    pallas_call x1, Pallas kernels, body(): pl.pallas_call(attend_kernel, out_shape=jax.ShapeDtypeStruct((8, 256, 128...  44.8 us
    pallas_call x1, Pallas kernels, body(): pl.pallas_call(return_kernel, out_shape=jax.ShapeDtypeStruct((ROWS, 1024)...  19.1 us
    unnamed x4, local copies, waits for them, and re-layouts  3.78 us

profile of v1, /device:TPU:9, one launch (start us, length us, event | category | flops | bytes accessed | tf_op | source)
XLA Modules:
  0.0 150.3 jit_solution(8958210047620862143)
XLA Ops:
  0.0 0.8 reduce-window.8
  0.9 0.0 copy-start
  0.9 0.2 select_reduce_fusion.1
  1.1 1.1 convert_reduce_fusion
  2.3 0.1 fusion.1
  2.4 0.4 select_reduce_fusion
  2.8 0.7 select_select_fusion.meta
  3.5 1.3 broadcast_in_dim.126.gain
  4.8 0.5 fusion.6
  5.3 1.0 pad_maximum_fusion
  6.3 1.9 %copy.12.tok = bf16[256,720]{1,0:T(8,128)(2,1)} copy(bf16[256,720]{0,1:T(8,128)(2,1)} %param.8) | data formatting | bytes 737280 | tf_op args[0]
  8.2 76.2 %project.1 = (bf16[64,256,128]{2,1,0:T(8,128)(2,1)}, bf16[8,256,128]{2,1,0:T(8,128)(2,1)}) custom-call(bf16[256,720]{1,0:T(8,128)(2,1)} %copy.12.tok, f32[1,2880]{1,0:T(1,128)} %broadcast_in_dim.126.gain, f32[256,128]{1,0:T(8,128)} %get-tuple-element.25.cos, f32[256,128]{1,0:T(8,128)} %get-tuple-element.26.sin, bf16[2880,1024]{1,0:T(8,128)(2,1)} %wq_hbm.1, ...), custom_call_target="tpu_custom_call" | custom-call | tf_op jit(solution)/shard_map/project/pallas_call | solution.py:360
  84.4 0.0 copy-done
  84.4 44.8 %attend.1.o_ref = bf16[8,256,128]{2,1,0:T(8,128)(2,1)} custom-call(s32[16,128]{1,0:T(8,128)} %select_select_fusion.meta, s32[12]{0:T(128)} %bitcast.4, f32[16]{0:T(128)} %sinks.1, bf16[8,256,128]{2,1,0:T(8,128)(2,1)} %get-tuple-element.7.q_ref, bf16[64,256,128]{2,1,0:T(8,128)(2,1)} %get-tuple-element.8.kv_ref), custom_call_target="tpu_custom_call" | custom-call | tf_op jit(solution)/shard_map/attend/pallas_call | solution.py:376
  129.3 19.1 %give_back.1 = bf16[256,1024]{1,0:T(8,128)(2,1)} custom-call(bf16[8,256,128]{2,1,0:T(8,128)(2,1)} %attend.1.o_ref), custom_call_target="tpu_custom_call" | custom-call | tf_op jit(solution)/shard_map/give_back/pallas_call | solution.py:384
  148.4 1.9 %copy.14 = bf16[256,1024]{1,0:T(8,128)(2,1)} copy(bf16[256,1024]{1,0:T(8,128)(2,1)} %give_back.1) | data formatting | bytes 1048576
  (8 shorter events, 0.1 us)
Async XLA Ops:
  0.9 83.6 %copy-start = (s32[12,1]{0,1:T(1,128)}, s32[12,1]{0,1:T(1,128)S(1)}, u32[]{:S(2)}) copy-start(s32[12,1]{0,1:T(1,128)S(1)} %reduce-window.8) | copy-start | bytes 148
